TPU v7x, 512 devices: a whole 4x4x16 slice. The times are simulated.
512 devices in a mesh: group: 32 (over x, y, core), tp: 16 (over z).
Axes of the slice: x: 4, y: 4, z: 16, core: 2. Of those that a mesh axis runs over, the one named last changes fastest.
Arguments:
- tokens: bfloat16 [24576, 8192], P('group', 'tp'), may hold values from -6 to 6
- w_query: bfloat16 [8192, 4096], P(None, 'tp'), may hold values from -0.0625 to 0.0625
- adapter_down: bfloat16 [384, 16, 8192], P('group', None, 'tp'), may hold values from -0.0625 to 0.0625
- adapter_up: bfloat16 [384, 16, 4096], P('group', None, 'tp'), may hold values from -1.5 to 1.5
- adapter_id: int32 [24576], P('group'), may hold values from 0 to 383, as said below
Outputs:
- query: bfloat16 [24576, 4096], P('group', 'tp')
Inputs may be any that keep to these rules, and one draw needn't show every extreme that they name: `adapter_id`: adapter a is owned by group a // 12. Among the 768 requests of one group (an aligned block), at most 48 use adapters of any one owner; in every draw one owner receives exactly 48 from every group.
All inputs are finite; a program needn't handle non-finite values.
Results may differ from a plain program's by a relative error of at most 0.014.
Values may be sent and summed in bfloat16 or wider, within the bound.
No kernel may reach another device: no remote copies, remote signals or barrier semaphores. Data moves between devices by JAX's collectives and lax.ppermute only.
A program may use at most 128 MiB of HBM per device.

v0:
```python
import jax
import jax.numpy as jnp
from jax import lax
from jax.sharding import PartitionSpec as P

adapter_scale_factor = 2.0
owner_slots = 48
F32, BF16 = (jnp.float32, jnp.bfloat16)


def slot_of_request(adapter_id, groups, per_group):
    n = adapter_id.shape[0]
    owner = adapter_id // per_group
    to_owner = owner[:, None] == lax.broadcasted_iota(jnp.int32, (n, groups), 1)
    before = lax.broadcasted_iota(jnp.int32, (n, n), 0) > lax.broadcasted_iota(jnp.int32, (n, n), 1)
    count = jnp.dot(before.astype(BF16), to_owner.astype(BF16), preferred_element_type=F32)
    rank = jnp.sum(jnp.where(to_owner, count, 0.0), axis=1).astype(jnp.int32)
    return owner * owner_slots + rank


def lora(tokens, adapter_down, adapter_up, adapter_id, groups, tp):
    n, d = tokens.shape
    per_group, rank, _ = adapter_down.shape
    ho = adapter_up.shape[2]
    slots = groups * owner_slots
    slot = slot_of_request(adapter_id, groups, per_group)
    place = (lax.broadcasted_iota(jnp.int32, (slots, n), 0) == slot[None, :]).astype(BF16)
    out_rows = jnp.dot(place, tokens, preferred_element_type=F32).astype(BF16)
    local = (adapter_id % per_group).astype(BF16)
    out_ids = jnp.dot(place, local[:, None], preferred_element_type=F32).astype(BF16)
    out_ids = out_ids.reshape(groups, 1, owner_slots)
    out_ids = jnp.pad(out_ids, ((0, 0), (0, 7), (0, d - owner_slots)))
    sent = jnp.concatenate([out_rows.reshape(groups, owner_slots, d), out_ids], axis=1)
    here = lax.all_to_all(sent, "group", 0, 0, tiled=True)
    rows = here[:, :owner_slots].reshape(slots, d)
    ids = here[:, owner_slots, :owner_slots].astype(jnp.int32).reshape(1, 1, slots)
    mine = lax.broadcasted_iota(jnp.int32, (per_group, 1, slots), 0) == ids
    part = lax.dot_general(
        adapter_down.reshape(per_group * rank, d),
        rows,
        (((1,), (1,)), ((), ())),
        preferred_element_type=F32,
    ).reshape(per_group, rank, slots)
    part = jnp.sum(jnp.where(mine, part, 0.0), axis=0)
    share = rank // tp
    part = lax.all_to_all(part.astype(BF16).reshape(tp, share, slots), "tp", 0, 0, tiled=True)
    scaled = (adapter_scale_factor * jnp.sum(part.astype(F32), axis=0)).astype(BF16)
    scaled = lax.all_to_all(
        jnp.broadcast_to(scaled[None], (tp, share, slots)), "tp", 0, 0, tiled=True
    ).reshape(1, rank, slots)
    spread = jnp.where(mine, scaled, jnp.zeros((), BF16)).reshape(per_group * rank, slots)
    delta = lax.dot_general(
        spread,
        adapter_up.reshape(per_group * rank, ho),
        (((0,), (0,)), ((), ())),
        preferred_element_type=F32,
    ).astype(BF16)
    delta = lax.all_to_all(delta.reshape(groups, owner_slots, ho), "group", 0, 0, tiled=True)
    return lax.dot_general(
        place, delta.reshape(slots, ho), (((0,), (0,)), ((), ())), preferred_element_type=F32
    ).astype(BF16)


def solution(mesh):
    groups, tp = (mesh.shape["group"], mesh.shape["tp"])

    def on_device(tokens, w_query, adapter_down, adapter_up, adapter_id):
        gathered = lax.all_gather(tokens, "tp", axis=1, tiled=True)
        delta = lora(tokens, adapter_down, adapter_up, adapter_id, groups, tp)
        delta, gathered = lax.optimization_barrier((delta, gathered))
        base = lax.optimization_barrier(jnp.dot(gathered, w_query, preferred_element_type=F32))
        return (base + delta.astype(F32)).astype(BF16)

    placed = (
        P("group", "tp"),
        P(None, "tp"),
        P("group", None, "tp"),
        P("group", None, "tp"),
        P("group"),
    )
    return jax.shard_map(
        on_device, mesh=mesh, in_specs=placed, out_specs=P("group", "tp"), check_vma=False
    )
```

profile of v0, /device:TPU:1, one launch (start us, length us, event | category | flops | bytes accessed | tf_op | source)
XLA Modules:
  0.0 182.4 jit_solution(1290667721489595639)
XLA Ops:
  6.5 0.0 copy-start
  6.5 0.0 copy-start.1
  6.5 0.0 all-gather.2.cloned.1.call-start
  6.5 0.7 all-gather.2.cloned.1.call-update
  7.3 0.7 add_select_fusion.1
  8.0 0.4 fusion.13
  8.3 0.7 convert_add_fusion
  9.0 0.9 fusion.14
  9.9 0.1 reshape.91
  10.0 0.0 copy-done.1
  10.0 1.4 fusion.4
  11.4 0.1 fusion.10
  11.6 35.1 %all_to_all.20 = bf16[32,56,512]{2,1,0:T(8,128)(2,1)S(1)} all-to-all(bf16[32,56,512]{2,1,0:T(8,128)(2,1)S(1)} %fusion.10), channel_id=1, replica_groups=mesh['group'=32,'tp'=16] {'group'}, dimensions={0} | all-to-all | bytes 3670016 | tf_op jit(solution)/shard_map/all_to_all | solution.py:34
  46.7 0.1 fusion.20
  46.8 0.1 reshape.86
  46.8 0.2 slice.9
  47.0 0.0 copy-done
  47.0 0.7 fusion.24
  47.7 0.0 copy-start.2
  47.7 0.1 select_reduce_fusion
  47.9 0.5 broadcast.31
  48.4 0.7 reduce.7
  49.1 25.2 %all_to_all.21 = bf16[16,2,768]{2,1,0:T(2,128)(2,1)S(1)} all-to-all(bf16[16,2,768]{2,1,0:T(2,128)(2,1)S(1)} %reshape.99), channel_id=1, replica_groups=mesh['group'=32,'tp'=16] {'tp'}, dimensions={0} | all-to-all | bytes 98304 | tf_op jit(solution)/shard_map/all_to_all | solution.py:46
  74.3 0.1 convert_reduce_fusion
  74.5 0.1 broadcast_in_dim.48
  74.5 0.9 reduce.8
  75.5 15.6 %all_to_all.22 = bf16[16,2,768]{2,1,0:T(2,128)(2,1)S(1)} all-to-all(bf16[16,2,768]{2,1,0:T(2,128)(2,1)S(1)} %reshape.101), channel_id=1, replica_groups=mesh['group'=32,'tp'=16] {'tp'}, dimensions={0} | all-to-all | bytes 98304 | tf_op jit(solution)/shard_map/all_to_all | solution.py:48
  91.1 0.0 copy-done.2
  91.2 0.4 fusion.5
  91.6 19.7 %all_to_all.23 = bf16[32,48,256]{2,1,0:T(8,128)(2,1)S(1)} all-to-all(bf16[32,48,256]{2,1,0:T(8,128)(2,1)S(1)} %bitcast.30), channel_id=1, replica_groups=mesh['group'=32,'tp'=16] {'group'}, dimensions={0} | all-to-all | bytes 1572864 | tf_op jit(solution)/shard_map/all_to_all | solution.py:58
  111.3 1.4 fusion.11
  112.7 54.4 %all-gather.2.cloned.1.call-done = bf16[768,8192]{1,0:T(8,128)(2,1)} async-done(((bf16[768,512]{1,0:T(8,128)(2,1)}), bf16[768,8192]{1,0:T(8,128)(2,1)}) %all-gather.2.cloned.1.call-update) | async-done | bytes 12582928 | tf_op jit(solution)/shard_map/all_gather | solution.py:68
  167.0 7.6 %fusion.25 = f32[768,256]{1,0:T(8,128)S(1)} fusion(bf16[768,8192]{1,0:T(8,128)(2,1)} %all-gather.2.cloned.1.call-done, bf16[8192,256]{1,0:T(8,128)(2,1)} %param.6), kind=kOutput, calls=%fused_computation.43 | convolution fusion | flops 3221225472 | bytes 17563648 | tf_op jit(solution)/shard_map/dot_general | solution.py:71
  174.7 0.9 add_convert_fusion
  (8 shorter events, 0.2 us)
Async XLA Ops:
  6.5 40.5 %copy-start = (bf16[12,16,512]{2,1,0:T(8,128)(2,1)S(1)}, bf16[12,16,512]{2,1,0:T(8,128)(2,1)}, u32[]{:S(2)}) copy-start(bf16[12,16,512]{2,1,0:T(8,128)(2,1)} %param.7) | copy-start | bytes 589828
  6.5 3.5 %copy-start.1 = (bf16[768,512]{1,0:T(8,128)(2,1)S(1)}, bf16[768,512]{1,0:T(8,128)(2,1)}, u32[]{:S(2)}) copy-start(bf16[768,512]{1,0:T(8,128)(2,1)} %param.5) | copy-start | bytes 2359300
  6.5 160.5 %all-gather.2.cloned.1.call-start = ((), (), s32[]{:S(2)}) async-start(), calls=%async_computation.4 | async-start | bytes 13369344 | tf_op jit(solution)/shard_map/all_gather | solution.py:68
  47.7 43.5 %copy-start.2 = (bf16[12,16,256]{2,1,0:T(8,128)(2,1)S(1)}, bf16[12,16,256]{2,1,0:T(8,128)(2,1)}, u32[]{:S(2)}) copy-start(bf16[12,16,256]{2,1,0:T(8,128)(2,1)} %param.8) | copy-start | bytes 294916
Sparse Core Ops, SparseCore 0:
  9.4 157.5 all-gather.1
where the time goes:
time: 183 us; the launch traced here: 182 us
  blocking collectives  95.6 us (52%)
  waiting for transfers between devices  55.1 us (30%)
  between operations  13.6 us (7%)
  matrix products  12.8 us (7%)
  other arithmetic  4.3 us (2%)
    all_gather x1, waiting for transfers between devices, on_device(): gathered = lax.all_gather(tokens, 'tp', axis=1, tiled=True)  54.4 us
    all_to_all x1, blocking collectives, lora(): here = lax.all_to_all(sent, 'group', 0, 0, tiled=True)  35.1 us
    all_to_all x1, blocking collectives, lora(): lax.all_to_all(part.astype(BF16).reshape(tp, share, slots), 'tp', 0, 0, t...  25.2 us
    all_to_all x1, blocking collectives, lora(): lax.all_to_all(delta.reshape(groups, owner_slots, ho), 'group', 0, 0, til...  19.7 us
    all_to_all x1, blocking collectives, lora(): lax.all_to_all(jnp.broadcast_to(scaled[None], (tp, share, slots)), 'tp',...  15.6 us
    dot_general x1, matrix products, on_device(): jnp.dot(gathered, w_query, preferred_element_type=F32)  7.62 us
  transfers between devices with their start and end apart: 1, of which 1 were waited for; matrix products, arithmetic and copies ran while one was open for 5% of the time, Pallas kernels for 0%

commit v1 on v0

--- a/solution.py
+++ b/solution.py
@@ -65,7 +65,9 @@
     groups, tp = (mesh.shape["group"], mesh.shape["tp"])
 
     def on_device(tokens, w_query, adapter_down, adapter_up, adapter_id):
-        gathered = lax.all_gather(tokens, "tp", axis=1, tiled=True)
+        gathered = jnp.concatenate(
+            lax.all_to_all(jnp.stack([tokens] * lax.axis_size("tp")), "tp", 0, 0), axis=1
+        )
         delta = lora(tokens, adapter_down, adapter_up, adapter_id, groups, tp)
         delta, gathered = lax.optimization_barrier((delta, gathered))
         base = lax.optimization_barrier(jnp.dot(gathered, w_query, preferred_element_type=F32))

time: 183 us -> 667 us (3.64)
  waiting for transfers between devices: 55.1 us -> 555 us
  blocking collectives: 95.6 us -> 74.9 us
  between operations: 13.6 us -> 0.19 us
  starting transfers between devices: 0.01 us -> 10.6 us
    all_to_all x0 -> x2, waiting for transfers between devices: none -> 555 us  [the longest x1 541 us: on_device(): lax.all_to_all(jnp.stack([tokens] * lax.axis_size('tp')), 'tp', 0, 0)]
    all_gather x1 -> x0, waiting for transfers between devices: 54.4 us -> none  [on_device(): gathered = lax.all_gather(tokens, 'tp', axis=1, tiled=True)]
    all_to_all x1 -> x0, blocking collectives: 19.7 us -> none  [lora(): lax.all_to_all(delta.reshape(groups, owner_slots, ho), 'group', 0, 0, til...]
    all_to_all x0 -> x2, starting transfers between devices: none -> 10.6 us  [the longest x1 5.68 us: lora(): lax.all_to_all(delta.reshape(groups, owner_slots, ho), 'group', 0, 0, til...]
  transfers between devices with their start and end apart: 1 -> 2, of which waited for: 1 -> 2; matrix products, arithmetic and copies ran while one was open for 5% -> 0% of each run, Pallas kernels for 0% -> 0%
where the time goes in v1:
time: 667 us; the launch traced here: 666 us
  waiting for transfers between devices  555 us (83%)
  blocking collectives  74.9 us (11%)
  matrix products  13.7 us (2%)
  starting transfers between devices  10.6 us (2%)
  local copies, waits for them, and re-layouts  7.01 us (1%)
    all_to_all x1, waiting for transfers between devices, on_device(): lax.all_to_all(jnp.stack([tokens] * lax.axis_size('tp')), 'tp', 0, 0)  541 us
    all_to_all x1, blocking collectives, lora(): here = lax.all_to_all(sent, 'group', 0, 0, tiled=True)  35.1 us
    all_to_all x1, blocking collectives, lora(): lax.all_to_all(part.astype(BF16).reshape(tp, share, slots), 'tp', 0, 0, t...  25.1 us
    all_to_all x1, blocking collectives, lora(): lax.all_to_all(jnp.broadcast_to(scaled[None], (tp, share, slots)), 'tp',...  14.7 us
    all_to_all x1, waiting for transfers between devices, lora(): lax.all_to_all(delta.reshape(groups, owner_slots, ho), 'group', 0, 0, til...  14 us
  transfers between devices with their start and end apart: 2, of which 2 were waited for; matrix products, arithmetic and copies ran while one was open for 0% of the time, Pallas kernels for 0%

profile of v1, /device:TPU:1, one launch (start us, length us, event | category | flops | bytes accessed | tf_op | source)
XLA Modules:
  0.0 666.1 jit_solution(725666950054029827)
XLA Ops:
  0.0 0.0 copy-start
  0.0 0.0 copy-start.1
  0.0 0.8 add_select_fusion.1
  0.8 0.4 fusion.13
  1.1 0.7 convert_add_fusion
  1.9 0.9 fusion.14
  2.8 0.1 reshape.101
  2.9 0.0 copy-done.1
  2.9 1.4 fusion.4
  4.3 0.1 fusion.10
  4.4 35.1 %all_to_all.25 = bf16[32,56,512]{2,1,0:T(8,128)(2,1)S(1)} all-to-all(bf16[32,56,512]{2,1,0:T(8,128)(2,1)S(1)} %fusion.10), channel_id=1, replica_groups=mesh['group'=32,'tp'=16] {'group'}, dimensions={0} | all-to-all | bytes 3670016 | tf_op jit(solution)/shard_map/all_to_all | solution.py:34
  39.5 0.1 fusion.20
  39.6 0.1 reshape.96
  39.7 0.2 slice.9
  39.9 0.0 copy-done
  39.9 0.7 fusion.24
  40.5 0.0 copy-start.2
  40.6 0.1 select_reduce_fusion
  40.7 0.5 broadcast.33
  41.2 0.7 reduce.7
  41.9 25.1 %all_to_all.26 = bf16[16,2,768]{2,1,0:T(2,128)(2,1)S(1)} all-to-all(bf16[16,2,768]{2,1,0:T(2,128)(2,1)S(1)} %reshape.109), channel_id=1, replica_groups=mesh['group'=32,'tp'=16] {'tp'}, dimensions={0} | all-to-all | bytes 98304 | tf_op jit(solution)/shard_map/all_to_all | solution.py:46
  67.0 0.1 convert_reduce_fusion
  67.1 0.1 broadcast_in_dim.48
  67.2 0.9 reduce.8
  68.1 14.7 %all_to_all.27 = bf16[16,2,768]{2,1,0:T(2,128)(2,1)S(1)} all-to-all(bf16[16,2,768]{2,1,0:T(2,128)(2,1)S(1)} %reshape.111), channel_id=1, replica_groups=mesh['group'=32,'tp'=16] {'tp'}, dimensions={0} | all-to-all | bytes 98304 | tf_op jit(solution)/shard_map/all_to_all | solution.py:48
  82.9 0.0 copy-done.2
  82.9 1.3 fusion.5
  84.2 5.7 all-to-all-start.3
  89.9 0.3 copy.12
  90.2 14.0 %all-to-all-done.3 = bf16[32,48,256]{2,1,0:T(8,128)(2,1)S(1)} async-done(((bf16[32,48,256]{2,1,0:T(8,128)(2,1)}), bf16[32,48,256]{2,1,0:T(8,128)(2,1)S(1)}, u32[]{:S(2)}, u32[]{:S(2)}) %all-to-all-start.3) | async-done | bytes 786464 | tf_op jit(solution)/shard_map/all_to_all | solution.py:58
  104.2 5.7 stack.2
  109.9 4.9 all-to-all-start.4
  114.9 1.4 fusion.11
  116.3 541.3 %all-to-all-done.4 = bf16[16,768,512]{1,2,0:T(8,128)(2,1)} async-done(((bf16[16,768,512]{1,2,0:T(8,128)(2,1)}), bf16[16,768,512]{1,2,0:T(8,128)(2,1)}, u32[]{:S(2)}, u32[]{:S(2)}) %all-to-all-start.4) | async-done | bytes 12582944 | tf_op jit(solution)/shard_map/all_to_all | solution.py:69
  657.6 7.7 %fusion.25 = f32[768,256]{1,0:T(8,128)S(1)} fusion(bf16[768,8192]{0,1:T(8,128)(2,1)} %bitcast.10, bf16[8192,256]{1,0:T(8,128)(2,1)} %param.6), kind=kOutput, calls=%fused_computation.43 | convolution fusion | flops 3221225472 | bytes 17563648 | tf_op jit(solution)/shard_map/dot_general | solution.py:73
  665.2 0.9 add_convert_fusion
  (8 shorter events, 0.2 us)
Async XLA Ops:
  0.0 39.9 %copy-start = (bf16[12,16,512]{2,1,0:T(8,128)(2,1)S(1)}, bf16[12,16,512]{2,1,0:T(8,128)(2,1)}, u32[]{:S(2)}) copy-start(bf16[12,16,512]{2,1,0:T(8,128)(2,1)} %param.7) | copy-start | bytes 589828
  0.0 2.9 copy-start.1
  40.5 42.4 %copy-start.2 = (bf16[12,16,256]{2,1,0:T(8,128)(2,1)S(1)}, bf16[12,16,256]{2,1,0:T(8,128)(2,1)}, u32[]{:S(2)}) copy-start(bf16[12,16,256]{2,1,0:T(8,128)(2,1)} %param.8) | copy-start | bytes 294916
  84.2 20.0 %all-to-all-start.3 = ((bf16[32,48,256]{2,1,0:T(8,128)(2,1)}), bf16[32,48,256]{2,1,0:T(8,128)(2,1)S(1)}, u32[]{:S(2)}, u32[]{:S(2)}) async-start(bf16[32,48,256]{2,1,0:T(8,128)(2,1)} %bitcast.7), calls=%async_computation.3 | async-start | bytes 1572864 | tf_op jit(solution)/shard_map/all_to_all | solution.py:58
  109.9 547.6 %all-to-all-start.4 = ((bf16[16,768,512]{1,2,0:T(8,128)(2,1)}), bf16[16,768,512]{1,2,0:T(8,128)(2,1)}, u32[]{:S(2)}, u32[]{:S(2)}) async-start(bf16[16,768,512]{1,2,0:T(8,128)(2,1)} %stack.2), calls=%async_computation.4 | async-start | bytes 25165824 | tf_op jit(solution)/shard_map/all_to_all | solution.py:69
